TPU v7x, 256 devices: a whole 4x4x8 slice. The times are simulated.
256 devices in a mesh: dp: 16 (over y, x_hi, core), mp: 16 (over z, x_lo).
Axes of the slice: x: 4 (x_hi: 2, x_lo: 2; x = x_hi * 2 + x_lo), y: 4, z: 8, core: 2. Of those that a mesh axis runs over, the one named last changes fastest.
Arguments:
- tokens: bfloat16 [16384, 2048], P(('dp', 'mp')), may hold values from -6 to 6
- norm_gain: float32 [2048], replicated, may hold values from 0.1 to 1.9
- mlp_gain: float32 [2048], replicated, may hold values from 0.1 to 1.9
- lengths: int32 [16], P('dp'), may hold values from 1 to 1024, as said below
- log_decay: float32 [16384, 8], P('dp'), as said below
- query_master: float32 [2048, 2048], P(('dp', 'mp')), may hold values from -0.125 to 0.125
- key_master: float32 [2048, 2048], P(('dp', 'mp')), may hold values from -0.125 to 0.125
- value_master: float32 [2048, 4096], P(('dp', 'mp')), may hold values from -0.125 to 0.125
- swish_master: float32 [2048, 4096], P(('dp', 'mp')), may hold values from -0.125 to 0.125
- output_master: float32 [4096, 2048], P(None, ('dp', 'mp')), may hold values from -0.09375 to 0.09375
- ffn_gate_master: float32 [2048, 4096], P(('dp', 'mp')), may hold values from -0.125 to 0.125
- ffn_up_master: float32 [2048, 4096], P(('dp', 'mp')), may hold values from -0.125 to 0.125
Outputs:
- residual: bfloat16 [16384, 2048], P(('dp', 'mp'))
- hidden: bfloat16 [16384, 4096], P('dp', 'mp')
Inputs may be any that keep to these rules, and one draw needn't show every extreme that they name: `lengths`: given length of each prompt; in every draw some prompt has exactly 1024 tokens and some has 1. `log_decay`: Negative.
All inputs are finite; a program needn't handle non-finite values.
Results may differ from a plain program's by a relative error of at most 0.023.
Values may be sent and summed in bfloat16 or wider, within the bound.
A program may use at most 128 MiB of HBM per device.

v0:
```python
import math
import jax
import jax.numpy as jnp
from jax import lax
from jax.sharding import PartitionSpec as P

H = 8
DK = 256
DV = 512
REQUEST_SPAN = 1024
BLOCK = 512
PROMPTS_DP = 1


def rms_rows(row_block, gain_vec):
    values = row_block.astype(jnp.float32)
    scale = lax.rsqrt(jnp.mean(values * values, axis=-1, keepdims=True) + 1e-06)
    return (values * scale * gain_vec).astype(jnp.bfloat16)


def rotate(values, places):
    columns = values.shape[1]
    channel = jnp.arange(columns, dtype=jnp.int32) % DK
    paired = (channel // 2 * 2).astype(jnp.float32)
    frequency = jnp.exp(paired * (-math.log(10000.0) / DK))
    angles = places.astype(jnp.float32)[:, None] * frequency[None, :]
    couples = values.reshape(values.shape[0], columns // 2, 2)
    turned = jnp.stack([-couples[:, :, 1], couples[:, :, 0]], axis=-1).reshape(values.shape)
    return values * jnp.cos(angles) + turned * jnp.sin(angles)


def spread_heads(matrix, width, copies):
    row_total = matrix.shape[0]
    per_head = jnp.repeat(matrix.reshape(row_total, H, width), copies, axis=1)
    return per_head.reshape(row_total, H * copies * width)


def trainer_order(block_rows, dp_count, mp_count):
    row_total, columns = block_rows.shape
    split_rows = block_rows.reshape(mp_count, dp_count, row_total // (dp_count * mp_count), columns)
    return split_rows.transpose(1, 0, 2, 3).reshape(row_total, columns)


def retain_block(offset, q_block, k_block, v_block, run_query, run_key):
    scores = jnp.einsum(
        "thd,shd->hts", q_block, k_block, preferred_element_type=jnp.float32
    ) * DK ** (-0.5)
    decay_gap = run_query.T[:, :, None] - run_key.T[:, None, :]
    causal_mask = (offset + jnp.arange(q_block.shape[0], dtype=jnp.int32))[:, None] >= jnp.arange(
        k_block.shape[0], dtype=jnp.int32
    )[None, :]
    weights = (scores * jnp.exp(jnp.where(causal_mask[None], decay_gap, -jnp.inf))).astype(
        jnp.bfloat16
    )
    return jnp.einsum("hts,shd->thd", weights, v_block, preferred_element_type=jnp.float32)


def per_device(
    tokens,
    norm_gain,
    mlp_gain,
    lengths,
    log_decay,
    query_master,
    key_master,
    value_master,
    swish_master,
    output_master,
    ffn_gate_master,
    ffn_up_master,
):
    mp_count = lax.axis_size("mp")
    dp_count = lax.axis_size("dp")
    mp_index = lax.axis_index("mp")
    head_share = max(1, mp_count // H)
    local_heads = max(1, H // mp_count)
    partner_bit = mp_index % head_share
    group_rows = PROMPTS_DP * REQUEST_SPAN
    value_width = DV // head_share
    m_query = spread_heads(query_master.astype(jnp.bfloat16), DK, head_share)
    m_key = spread_heads(key_master.astype(jnp.bfloat16), DK, head_share)
    m_value = spread_heads(value_master.astype(jnp.bfloat16), DV, head_share)
    m_swish = swish_master.astype(jnp.bfloat16)
    m_output = output_master.T.astype(jnp.bfloat16)
    m_ffn_gate = ffn_gate_master.astype(jnp.bfloat16)
    m_ffn_up = ffn_up_master.astype(jnp.bfloat16)
    r_query, r_key, r_value, r_swish, r_output, r_gate, r_up = (
        lax.all_gather(m_query, "dp", axis=0, tiled=True),
        lax.all_gather(m_key, "dp", axis=0, tiled=True),
        lax.all_gather(m_value, "dp", axis=0, tiled=True),
        lax.all_gather(m_swish, "dp", axis=0, tiled=True),
        lax.all_gather(m_output, "dp", axis=0, tiled=True),
        lax.all_gather(m_ffn_gate, "dp", axis=0, tiled=True),
        lax.all_gather(m_ffn_up, "dp", axis=0, tiled=True),
    )
    owned_parts = (
        lax.all_to_all(r_query, "mp", split_axis=1, concat_axis=0, tiled=True),
        lax.all_to_all(r_key, "mp", split_axis=1, concat_axis=0, tiled=True),
        lax.all_to_all(r_value, "mp", split_axis=1, concat_axis=0, tiled=True),
        lax.all_to_all(r_swish, "mp", split_axis=1, concat_axis=0, tiled=True),
        lax.all_to_all(r_output, "mp", split_axis=1, concat_axis=0, tiled=True),
        lax.all_to_all(r_gate, "mp", split_axis=1, concat_axis=0, tiled=True),
        lax.all_to_all(r_up, "mp", split_axis=1, concat_axis=0, tiled=True),
    )
    server = [trainer_order(owned, dp_count, mp_count) for owned in owned_parts]
    w_query, w_key, w_value, w_swish, w_output, w_ffn_gate, w_ffn_up = server
    width_qk = w_query.shape[1]
    width_value = w_value.shape[1]
    merged_weights = jnp.concatenate([w_query, w_key, w_value, w_swish], axis=1)
    normed_in = rms_rows(tokens, norm_gain)
    shard_piece = lax.all_gather(normed_in, "mp", axis=0, tiled=True)
    places = jnp.arange(shard_piece.shape[0], dtype=jnp.int32) % REQUEST_SPAN
    projected_rows = jnp.dot(shard_piece, merged_weights, preferred_element_type=jnp.float32)
    rotated_query = rotate(projected_rows[:, :width_qk], places)
    rotated_key = rotate(projected_rows[:, width_qk : 2 * width_qk], places)
    projected = jnp.concatenate(
        [rotated_query, rotated_key, projected_rows[:, 2 * width_qk :]], axis=1
    ).astype(jnp.bfloat16)
    queries = projected[:, :width_qk]
    key_rows = projected[:, width_qk : 2 * width_qk]
    value_rows = projected[:, 2 * width_qk : 2 * width_qk + width_value]
    gate_rows = projected[:, 2 * width_qk + width_value :]
    head_first = mp_index // head_share * local_heads
    decay_cols = lax.dynamic_slice_in_dim(log_decay, head_first, local_heads, 1)
    running = jnp.cumsum(decay_cols.reshape(PROMPTS_DP, REQUEST_SPAN, local_heads), axis=1)
    query_four = queries.reshape(PROMPTS_DP, REQUEST_SPAN, local_heads, DK)
    key_four = key_rows.reshape(PROMPTS_DP, REQUEST_SPAN, local_heads, DK)
    value_four = value_rows.reshape(PROMPTS_DP, REQUEST_SPAN, local_heads, DV)

    def one_prompt(prompt_items):
        q_prompt, k_prompt, v_prompt, run_prompt, length_prompt = prompt_items
        outputs = []
        for block_index in range(REQUEST_SPAN // BLOCK):
            low_row = block_index * BLOCK
            top_row = low_row + BLOCK
            operands = (
                q_prompt[low_row:top_row],
                k_prompt[:top_row],
                v_prompt[:top_row],
                run_prompt[low_row:top_row],
                run_prompt[:top_row],
            )
            block_out = retain_block(low_row, *operands)
            outputs.append(block_out)
        return jnp.concatenate(outputs, axis=0)

    retained = lax.map(one_prompt, (query_four, key_four, value_four, running, lengths))
    retained = retained.reshape(group_rows, local_heads, DV)
    channel_mean = jnp.mean(retained, axis=-1, keepdims=True)
    spread = jnp.mean(retained * retained, axis=-1, keepdims=True) - channel_mean * channel_mean
    normed_heads = (retained - channel_mean) * lax.rsqrt(spread + 1e-05)
    normed_heads = lax.dynamic_slice_in_dim(normed_heads, partner_bit * value_width, value_width, 2)
    live_rows = jnp.arange(group_rows, dtype=jnp.int32) % REQUEST_SPAN < jnp.repeat(
        lengths, REQUEST_SPAN
    )
    gated = jnp.where(
        live_rows[:, None],
        jax.nn.silu(gate_rows.astype(jnp.float32))
        * normed_heads.reshape(group_rows, local_heads * value_width),
        0.0,
    ).astype(jnp.bfloat16)
    branch = lax.psum_scatter(
        lax.dot_general(
            gated, w_output, (((1,), (1,)), ((), ())), preferred_element_type=jnp.float32
        ).astype(jnp.bfloat16),
        "mp",
        scatter_dimension=0,
        tiled=True,
    ).astype(jnp.float32)
    residual = (tokens.astype(jnp.float32) + branch).astype(jnp.bfloat16)
    normed_mid = rms_rows(residual, mlp_gain)
    w_gate_up = jnp.concatenate([w_ffn_gate, w_ffn_up], axis=1)
    split_at = w_ffn_gate.shape[1]
    gate_up = jnp.dot(
        lax.all_gather(normed_mid, "mp", axis=0, tiled=True),
        w_gate_up,
        preferred_element_type=jnp.float32,
    )
    hidden = (jax.nn.silu(gate_up[:, :split_at]) * gate_up[:, split_at:]).astype(jnp.bfloat16)
    return (residual, hidden)


def solution(mesh):
    placed = (
        P(("dp", "mp"), None),
        P(),
        P(),
        P("dp"),
        P("dp", None),
        P(("dp", "mp"), None),
        P(("dp", "mp"), None),
        P(("dp", "mp"), None),
        P(("dp", "mp"), None),
        P(None, ("dp", "mp")),
        P(("dp", "mp"), None),
        P(("dp", "mp"), None),
    )
    return jax.shard_map(
        per_device,
        mesh=mesh,
        in_specs=placed,
        out_specs=(P(("dp", "mp"), None), P("dp", "mp")),
        check_vma=False,
    )
```

profile of v0, /device:TPU:1, one launch (start us, length us, event | category | flops | bytes accessed | tf_op | source)
XLA Modules:
  0.0 776.2 jit_solution(15187290181166123529)
XLA Ops:
  7.2 0.9 convert_element_type.97
  8.1 0.6 broadcast_in_dim.61
  8.8 0.8 convert_element_type.96
  10.4 1.5 convert_element_type.99
  12.0 1.5 convert_bitcast_fusion
  13.5 52.0 %all-gather.14.cloned.1.call-done = bf16[128,4096]{1,0:T(8,128)(2,1)} async-done(((bf16[8,4096]{1,0:T(8,128)(2,1)}), bf16[128,4096]{1,0:T(8,128)(2,1)}) %all-gather.14.cloned.1.call-update) | async-done | bytes 1048592 | tf_op jit(solution)/shard_map/all_gather | solution.py:89
  65.5 2.3 copy.66
  67.8 6.8 all-to-all-start.1
  74.7 0.7 broadcast_in_dim.62
  75.4 41.6 %all-gather.12.cloned.1.call-done = bf16[128,4096]{1,0:T(8,128)(2,1)} async-done(((bf16[8,4096]{1,0:T(8,128)(2,1)}), bf16[128,4096]{1,0:T(8,128)(2,1)}) %all-gather.12.cloned.1.call-update) | async-done | bytes 1048592 | tf_op jit(solution)/shard_map/all_gather | solution.py:88
  117.0 2.3 copy.63
  119.3 6.8 all-to-all-start
  126.3 42.8 %all-gather.18.cloned.1.call-done = bf16[128,4096]{1,0:T(8,128)(2,1)} async-done(((bf16[8,4096]{1,0:T(8,128)(2,1)}), bf16[128,4096]{1,0:T(8,128)(2,1)}) %all-gather.18.cloned.1.call-update) | async-done | bytes 1048592 | tf_op jit(solution)/shard_map/all_gather | solution.py:91
  169.1 2.3 copy.72
  171.4 6.8 all-to-all-start.3
  178.3 0.8 fusion.48
  179.1 41.3 %all-gather.20.cloned.1.call-done = bf16[128,4096]{1,0:T(8,128)(2,1)} async-done(((bf16[8,4096]{1,0:T(8,128)(2,1)}), bf16[128,4096]{1,0:T(8,128)(2,1)}) %all-gather.20.cloned.1.call-update) | async-done | bytes 1048592 | tf_op jit(solution)/shard_map/all_gather | solution.py:92
  220.4 2.3 copy.79
  222.7 6.9 all-to-all-start.4
  229.6 45.4 %all-gather.16.cloned.1.call-done = bf16[128,8192]{1,0:T(8,128)(2,1)} async-done(((bf16[8,8192]{1,0:T(8,128)(2,1)}), bf16[128,8192]{1,0:T(8,128)(2,1)}) %all-gather.16.cloned.1.call-update) | async-done | bytes 2097168 | tf_op jit(solution)/shard_map/all_gather | solution.py:90
  275.0 4.1 copy.69
  279.1 6.8 all-to-all-start.2
  287.7 1.3 copy.67
  289.0 2.4 copy.68
  291.4 1.3 copy.64
  292.8 2.4 copy.65
  295.1 1.3 copy.73
  296.5 2.4 copy.74
  298.8 1.5 copy.80
  300.3 1.1 copy.81
  301.4 49.0 %all-to-all-done.2 = bf16[128,16,512]{0,2,1:T(8,128)(2,1)S(1)} async-done(((bf16[128,16,512]{0,2,1:T(8,128)(2,1)}), bf16[128,16,512]{0,2,1:T(8,128)(2,1)S(1)}, u32[]{:S(2)}, u32[]{:S(2)}) %all-to-all-start.2) | async-done | bytes 2097184 | tf_op jit(solution)/shard_map/all_to_all | solution.py:99
  350.4 2.6 copy.70
  353.0 1.9 copy.71
  354.9 52.4 %all-gather.10.cloned.1.call-done = bf16[1024,2048]{1,0:T(8,128)(2,1)} async-done(((bf16[64,2048]{1,0:T(8,128)(2,1)}), bf16[1024,2048]{1,0:T(8,128)(2,1)}) %all-gather.10.cloned.1.call-update) | async-done | bytes 4194320 | tf_op jit(solution)/shard_map/all_gather | solution.py:111
  407.3 9.9 %fusion.85 = (bf16[1024,1280]{1,0:T(8,128)(2,1)}, f32[1024,1280]{1,0:T(8,128)S(1)}) fusion(bf16[1024,2048]{1,0:T(8,128)(2,1)} %all-gather.10.cloned.1.call-done, bf16[2048,256]{1,0:T(8,128)(2,1)} %bitcast.111, bf16[2048,512]{1,0:T(8,128)(2,1)S(1)} %bitcast.107, bf16[2048,256]{1,0:T(8,128)(2,1)S(1)} %bitcast.109, bf16[2048,256]{1,0:T(8,128)(2,1)} %bitcast.110), kind=kOutput, calls=%fused_computation.126 | convolution fusion | flops 5390991360 | bytes 17301504 | tf_op jit(solution)/shard_map/dot_general | solution.py:113
  417.2 1.2 fusion.84
  418.4 1.4 copy-done.6
  420.8 0.8 slice_negate_fusion
  421.6 0.9 pad_maximum_fusion.2
  422.6 0.7 reshape.450
  423.6 1.6 copy.75
  425.8 0.8 slice_negate_fusion.1
  426.7 0.9 pad_maximum_fusion.1
  427.6 0.7 reshape.448
  428.7 7.1 fusion.25
  435.8 0.8 copy-done.12
  436.8 1.7 convolution_bitcast_fusion.1
  438.4 2.7 convolution_bitcast_fusion
  441.5 4.5 convolution_convert_fusion
  446.1 0.8 copy-done.15
  448.4 96.5 %reduce-scatter.2.cloned.1.call-done = bf16[64,2048]{1,0:T(8,128)(2,1)} async-done(((bf16[1024,2048]{1,0:T(8,128)(2,1)}), bf16[64,2048]{1,0:T(8,128)(2,1)}) %reduce-scatter.2.cloned.1.call-update) | async-done | bytes 262160 | tf_op jit(solution)/shard_map/reduce_scatter | solution.py:162
  544.9 1.1 fusion.43
  546.0 0.8 fusion.45
  546.9 52.9 %all-gather.24.cloned.1.call-done = bf16[128,4096]{1,0:T(8,128)(2,1)} async-done(((bf16[8,4096]{1,0:T(8,128)(2,1)}), bf16[128,4096]{1,0:T(8,128)(2,1)}) %all-gather.24.cloned.1.call-update) | async-done | bytes 1048592 | tf_op jit(solution)/shard_map/all_gather | solution.py:93
  599.8 2.3 copy.82
  602.1 6.8 all-to-all-start.5
  608.9 42.4 %all-gather.26.cloned.1.call-done = bf16[128,4096]{1,0:T(8,128)(2,1)} async-done(((bf16[8,4096]{1,0:T(8,128)(2,1)}), bf16[128,4096]{1,0:T(8,128)(2,1)}) %all-gather.26.cloned.1.call-update) | async-done | bytes 1048592 | tf_op jit(solution)/shard_map/all_gather | solution.py:94
  651.3 2.3 copy.85
  653.6 6.8 all-to-all-start.6
  661.0 1.1 copy.84
  662.1 31.7 %all-to-all-done.6 = bf16[128,16,256]{0,2,1:T(8,128)(2,1)S(1)} async-done(((bf16[128,16,256]{0,2,1:T(8,128)(2,1)}), bf16[128,16,256]{0,2,1:T(8,128)(2,1)S(1)}, u32[]{:S(2)}, u32[]{:S(2)}) %all-to-all-start.6) | async-done | bytes 1048608 | tf_op jit(solution)/shard_map/all_to_all | solution.py:103
  694.4 69.3 %all-gather.22.cloned.1.call-done = bf16[1024,2048]{1,0:T(8,128)(2,1)} async-done(((bf16[64,2048]{1,0:T(8,128)(2,1)}), bf16[1024,2048]{1,0:T(8,128)(2,1)}) %all-gather.22.cloned.1.call-update) | async-done | bytes 4194320 | tf_op jit(solution)/shard_map/all_gather | solution.py:175
  763.7 4.5 fusion.8
  768.2 1.1 fusion.32
  (91 shorter events, 7.6 us)
Async XLA Ops:
  7.2 278.9 %copy-start = (f32[1024,8]{0,1:T(8,128)S(1)}, f32[1024,8]{0,1:T(8,128)}, u32[]{:S(2)}) copy-start(f32[1024,8]{0,1:T(8,128)} %param.16) | copy-start | bytes 98308
  7.2 67.5 %copy-start.14 = (f32[8,4096]{1,0:T(8,128)S(1)}, f32[8,4096]{1,0:T(8,128)}, u32[]{:S(2)}) copy-start(f32[8,4096]{1,0:T(8,128)} %param.19) | copy-start | bytes 393220
  7.2 58.3 %all-gather.14.cloned.1.call-start = ((), (), s32[]{:S(2)}) async-start(), calls=%async_computation.10 | async-start | bytes 1114112 | tf_op jit(solution)/shard_map/all_gather | solution.py:89
  8.8 108.2 %all-gather.12.cloned.1.call-start = ((), (), s32[]{:S(2)}) async-start(), calls=%async_computation.9 | async-start | bytes 1114112 | tf_op jit(solution)/shard_map/all_gather | solution.py:88
  10.3 158.7 %all-gather.18.cloned.1.call-start = ((), (), s32[]{:S(2)}) async-start(), calls=%async_computation.12 | async-start | bytes 1114112 | tf_op jit(solution)/shard_map/all_gather | solution.py:91
  11.9 208.5 %all-gather.20.cloned.1.call-start = ((), (), s32[]{:S(2)}) async-start(), calls=%async_computation.13 | async-start | bytes 1114112 | tf_op jit(solution)/shard_map/all_gather | solution.py:92
  67.8 51.5 %all-to-all-start.1 = ((bf16[128,16,256]{0,2,1:T(8,128)(2,1)}), bf16[128,16,256]{0,2,1:T(8,128)(2,1)S(1)}, u32[]{:S(2)}, u32[]{:S(2)}) async-start(bf16[128,16,256]{0,2,1:T(8,128)(2,1)} %bitcast.10), calls=%async_computation.1 | async-start | bytes 2097152 | tf_op jit(solution)/shard_map/all_to_all | solution.py:98
  74.6 51.5 %copy-start.7 = (bf16[64,2048]{1,0:T(8,128)(2,1)S(1)}, bf16[64,2048]{1,0:T(8,128)(2,1)}, u32[]{:S(2)}) copy-start(bf16[64,2048]{1,0:T(8,128)(2,1)} %param.12) | copy-start | bytes 786436
  74.7 200.4 %all-gather.16.cloned.1.call-start = ((), (), s32[]{:S(2)}) async-start(), calls=%async_computation.11 | async-start | bytes 2228224 | tf_op jit(solution)/shard_map/all_gather | solution.py:90
  119.3 52.1 %all-to-all-start = ((bf16[128,16,256]{0,2,1:T(8,128)(2,1)}), bf16[128,16,256]{0,2,1:T(8,128)(2,1)S(1)}, u32[]{:S(2)}, u32[]{:S(2)}) async-start(bf16[128,16,256]{0,2,1:T(8,128)(2,1)} %bitcast.3), calls=%async_computation | async-start | bytes 2097152 | tf_op jit(solution)/shard_map/all_to_all | solution.py:97
  126.1 52.1 %copy-start.17 = (f32[2048]{0:T(1024)S(1)}, f32[2048]{0:T(1024)}, u32[]{:S(2)}) copy-start(f32[2048]{0:T(1024)} %param.13) | copy-start | bytes 24580
  171.4 51.3 %copy-start.2 = (bf16[128,16,256]{0,2,1:T(8,128)(2,1)}, bf16[128,16,256]{0,2,1:T(8,128)(2,1)S(1)}, u32[]{:S(2)}) copy-start(bf16[128,16,256]{0,2,1:T(8,128)(2,1)S(1)} %all-to-all-done) | copy-start | bytes 3145732
  171.4 51.3 %all-to-all-start.3 = ((bf16[128,16,256]{0,2,1:T(8,128)(2,1)}), bf16[128,16,256]{0,2,1:T(8,128)(2,1)S(1)}, u32[]{:S(2)}, u32[]{:S(2)}) async-start(bf16[128,16,256]{0,2,1:T(8,128)(2,1)} %bitcast.97), calls=%async_computation.3 | async-start | bytes 2097152 | tf_op jit(solution)/shard_map/all_to_all | solution.py:100
  178.2 229.1 %all-gather.10.cloned.1.call-start = ((), (), s32[]{:S(2)}) async-start(), calls=%async_computation.8 | async-start | bytes 4456448 | tf_op jit(solution)/shard_map/all_gather | solution.py:111
  222.7 56.5 %copy-start.4 = (bf16[128,16,256]{0,2,1:T(8,128)(2,1)}, bf16[128,16,256]{0,2,1:T(8,128)(2,1)S(1)}, u32[]{:S(2)}) copy-start(bf16[128,16,256]{0,2,1:T(8,128)(2,1)S(1)} %all-to-all-done.3) | copy-start | bytes 3145732
  222.7 56.5 %all-to-all-start.4 = ((bf16[128,16,256]{0,2,1:T(8,128)(2,1)}), bf16[128,16,256]{0,2,1:T(8,128)(2,1)}, u32[]{:S(2)}, u32[]{:S(2)}) async-start(bf16[128,16,256]{0,2,1:T(8,128)(2,1)} %bitcast.99), calls=%async_computation.4 | async-start | bytes 2097152 | tf_op jit(solution)/shard_map/all_to_all | solution.py:101
  279.1 71.3 %all-to-all-start.2 = ((bf16[128,16,512]{0,2,1:T(8,128)(2,1)}), bf16[128,16,512]{0,2,1:T(8,128)(2,1)S(1)}, u32[]{:S(2)}, u32[]{:S(2)}) async-start(bf16[128,16,512]{0,2,1:T(8,128)(2,1)} %bitcast.17), calls=%async_computation.2 | async-start | bytes 4194304 | tf_op jit(solution)/shard_map/all_to_all | solution.py:99
  286.0 258.9 %reduce-scatter.2.cloned.1.call-start = ((), (), s32[]{:S(2)}) async-start(), calls=%async_computation.14 | async-start | bytes 4456448 | tf_op jit(solution)/shard_map/reduce_scatter | solution.py:162
  289.0 2.4 copy-start.3
  292.7 2.4 copy-start.5
  353.0 54.3 %copy-start.9 = (bf16[16,16,8,256]{3,2,1,0:T(8,128)(2,1)S(1)}, bf16[16,16,8,256]{3,2,1,0:T(8,128)(2,1)}, u32[]{:S(2)}) copy-start(bf16[16,16,8,256]{3,2,1,0:T(8,128)(2,1)} %copy.68) | copy-start | bytes 3145732
  417.2 2.6 copy-start.6
  435.8 0.8 copy-start.12
  435.8 1.0 copy-start.13
  438.4 3.1 copy-start.8
  446.0 0.9 copy-start.15
  446.0 1.6 copy-start.16
  446.0 100.0 %copy-start.18 = (f32[2048]{0:T(1024)S(1)}, f32[2048]{0:T(1024)}, u32[]{:S(2)}) copy-start(f32[2048]{0:T(1024)} %param.14) | copy-start | bytes 24580
  446.1 153.7 %all-gather.24.cloned.1.call-start = ((), (), s32[]{:S(2)}) async-start(), calls=%async_computation.16 | async-start | bytes 1114112 | tf_op jit(solution)/shard_map/all_gather | solution.py:93
  447.6 203.7 %all-gather.26.cloned.1.call-start = ((), (), s32[]{:S(2)}) async-start(), calls=%async_computation.17 | async-start | bytes 1114112 | tf_op jit(solution)/shard_map/all_gather | solution.py:94
  448.3 315.4 %all-gather.22.cloned.1.call-start = ((), (), s32[]{:S(2)}) async-start(), calls=%async_computation.15 | async-start | bytes 4456448 | tf_op jit(solution)/shard_map/all_gather | solution.py:175
  546.0 56.1 %copy-start.11 = (bf16[64,2048]{1,0:T(8,128)(2,1)}, bf16[64,2048]{1,0:T(8,128)(2,1)S(1)}, u32[]{:S(2)}) copy-start(bf16[64,2048]{1,0:T(8,128)(2,1)S(1)} %get-tuple-element.17) | copy-start | bytes 786436
  602.1 51.5 %all-to-all-start.5 = ((bf16[128,16,256]{0,2,1:T(8,128)(2,1)}), bf16[128,16,256]{0,2,1:T(8,128)(2,1)S(1)}, u32[]{:S(2)}, u32[]{:S(2)}) async-start(bf16[128,16,256]{0,2,1:T(8,128)(2,1)} %bitcast.46), calls=%async_computation.6 | async-start | bytes 2097152 | tf_op jit(solution)/shard_map/all_to_all | solution.py:102
  653.6 40.2 %all-to-all-start.6 = ((bf16[128,16,256]{0,2,1:T(8,128)(2,1)}), bf16[128,16,256]{0,2,1:T(8,128)(2,1)S(1)}, u32[]{:S(2)}, u32[]{:S(2)}) async-start(bf16[128,16,256]{0,2,1:T(8,128)(2,1)} %bitcast.51), calls=%async_computation.7 | async-start | bytes 2097152 | tf_op jit(solution)/shard_map/all_to_all | solution.py:103
  662.1 101.7 %copy-start.10 = (bf16[16,16,8,256]{3,2,1,0:T(8,128)(2,1)S(1)}, bf16[16,16,8,256]{3,2,1,0:T(8,128)(2,1)}, u32[]{:S(2)}) copy-start(bf16[16,16,8,256]{3,2,1,0:T(8,128)(2,1)} %copy.84) | copy-start | bytes 3145732
  763.7 5.6 copy-start.1
Sparse Core Ops, SparseCore 0:
  11.4 54.1 all-gather.13
  68.3 48.6 all-gather.11
  120.3 48.6 all-gather.17
  171.7 48.6 all-gather.19
  223.6 51.4 all-gather.15
  277.2 130.0 all-gather.9
  446.2 98.6 reduce-scatter.1
  547.6 52.1 all-gather.23
  602.6 48.6 all-gather.25
  653.5 110.1 all-gather.21
where the time goes:
time: 778 us; the launch traced here: 776 us
  waiting for transfers between devices  617 us (79%)
  local copies, waits for them, and re-layouts  50.1 us (6%)
  starting transfers between devices  48.4 us (6%)
  matrix products  23.2 us (3%)
  other arithmetic  21.8 us (3%)
  between operations  15.3 us (2%)
    reduce_scatter x1, waiting for transfers between devices, per_device(): lax.psum_scatter(lax.dot_general(gated, w_output, (((1,), (1,)), ((), ())...  96.5 us
    all_gather x1, waiting for transfers between devices, per_device(): lax.all_gather(normed_mid, 'mp', axis=0, tiled=True)  69.3 us
    all_gather x1, waiting for transfers between devices, per_device(): lax.all_gather(m_ffn_gate, 'dp', axis=0, tiled=True)  52.9 us
    all_gather x1, waiting for transfers between devices, per_device(): shard_piece = lax.all_gather(normed_in, 'mp', axis=0, tiled=True)  52.4 us
    all_gather x1, waiting for transfers between devices, per_device(): lax.all_gather(m_key, 'dp', axis=0, tiled=True)  52 us
    all_to_all x1, waiting for transfers between devices, per_device(): lax.all_to_all(r_value, 'mp', split_axis=1, concat_axis=0, tiled=True)  49 us
    all_gather x1, waiting for transfers between devices, per_device(): lax.all_gather(m_value, 'dp', axis=0, tiled=True)  45.4 us
    all_gather x1, waiting for transfers between devices, per_device(): lax.all_gather(m_swish, 'dp', axis=0, tiled=True)  42.8 us
  transfers between devices with their start and end apart: 17, of which 12 were waited for; matrix products, arithmetic and copies ran while one was open for 6% of the time, Pallas kernels for 0%

commit v1 on v0

--- a/solution.py
+++ b/solution.py
@@ -88,7 +88,9 @@
         lax.all_gather(m_query, "dp", axis=0, tiled=True),
         lax.all_gather(m_key, "dp", axis=0, tiled=True),
         lax.all_gather(m_value, "dp", axis=0, tiled=True),
-        lax.all_gather(m_swish, "dp", axis=0, tiled=True),
+        jnp.concatenate(
+            lax.all_to_all(jnp.stack([m_swish] * lax.axis_size("dp")), "dp", 0, 0), axis=0
+        ),
         lax.all_gather(m_output, "dp", axis=0, tiled=True),
         lax.all_gather(m_ffn_gate, "dp", axis=0, tiled=True),
         lax.all_gather(m_ffn_up, "dp", axis=0, tiled=True),

time: 778 us -> 728 us (0.936)
  waiting for transfers between devices: 617 us -> 543 us
  blocking collectives: 0 us -> 25.9 us
    all_gather x1 -> x0, waiting for transfers between devices: 42.8 us -> none  [per_device(): lax.all_gather(m_swish, 'dp', axis=0, tiled=True)]
    all_gather x1, waiting for transfers between devices: 52 us -> 18.1 us  [per_device(): lax.all_gather(m_key, 'dp', axis=0, tiled=True)]
    all_to_all x0 -> x1, blocking collectives: none -> 25.9 us  [per_device(): lax.all_to_all(jnp.stack([m_swish] * lax.axis_size('dp')), 'dp', 0, 0)]
  transfers between devices with their start and end apart: 17 -> 16, of which waited for: 12 -> 12; matrix products, arithmetic and copies ran while one was open for 6% -> 6% of each run, Pallas kernels for 0% -> 0%
where the time goes in v1:
time: 728 us; the launch traced here: 726 us
  waiting for transfers between devices  543 us (75%)
  starting transfers between devices  50 us (7%)
  local copies, waits for them, and re-layouts  48.6 us (7%)
  blocking collectives  25.9 us (4%)
  matrix products  23.2 us (3%)
  other arithmetic  21.1 us (3%)
  between operations  15 us (2%)
    reduce_scatter x1, waiting for transfers between devices, per_device(): lax.psum_scatter(lax.dot_general(gated, w_output, (((1,), (1,)), ((), ())...  96.7 us
    all_gather x1, waiting for transfers between devices, per_device(): lax.all_gather(normed_mid, 'mp', axis=0, tiled=True)  69.9 us
    all_gather x1, waiting for transfers between devices, per_device(): shard_piece = lax.all_gather(normed_in, 'mp', axis=0, tiled=True)  54.4 us
    all_gather x1, waiting for transfers between devices, per_device(): lax.all_gather(m_ffn_gate, 'dp', axis=0, tiled=True)  51.9 us
    all_to_all x1, waiting for transfers between devices, per_device(): lax.all_to_all(r_value, 'mp', split_axis=1, concat_axis=0, tiled=True)  48.6 us
    all_gather x1, waiting for transfers between devices, per_device(): lax.all_gather(m_value, 'dp', axis=0, tiled=True)  45.4 us
    all_gather x1, waiting for transfers between devices, per_device(): lax.all_gather(m_ffn_up, 'dp', axis=0, tiled=True)  42.4 us
    all_gather x1, waiting for transfers between devices, per_device(): lax.all_gather(m_output, 'dp', axis=0, tiled=True)  41.4 us
  transfers between devices with their start and end apart: 16, of which 12 were waited for; matrix products, arithmetic and copies ran while one was open for 6% of the time, Pallas kernels for 0%

profile of v1, /device:TPU:1, one launch (start us, length us, event | category | flops | bytes accessed | tf_op | source)
XLA Modules:
  0.0 726.4 jit_solution(722321175579754053)
XLA Ops:
  7.2 0.8 convert_element_type.97
  8.8 0.8 convert_element_type.96
  10.3 1.5 convert_bitcast_fusion
  11.9 0.9 convert_element_type.99
  12.9 25.9 %all_to_all.117 = bf16[16,8,4096]{2,1,0:T(8,128)(2,1)S(1)} all-to-all(bf16[16,8,4096]{2,1,0:T(8,128)(2,1)S(1)} %stack.6), channel_id=1, replica_groups=mesh['dp'=16,'mp'=16] {'dp'}, dimensions={0} | all-to-all | bytes 2097152 | tf_op jit(solution)/shard_map/all_to_all | solution.py:92
  39.0 1.3 copy.73
  40.4 8.3 %all-to-all-start.4 = ((bf16[128,16,256]{2,0,1:T(8,128)(2,1)}), bf16[128,16,256]{2,0,1:T(8,128)(2,1)S(1)}, u32[]{:S(2)}, u32[]{:S(2)}) async-start(bf16[128,16,256]{2,0,1:T(8,128)(2,1)} %copy.73), calls=%async_computation.4 | async-start | bytes 2097152 | tf_op jit(solution)/shard_map/all_to_all | solution.py:102
  48.8 0.7 broadcast_in_dim.62
  49.5 18.1 %all-gather.13.cloned.1.call-done = bf16[128,4096]{1,0:T(8,128)(2,1)} async-done(((bf16[8,4096]{1,0:T(8,128)(2,1)}), bf16[128,4096]{1,0:T(8,128)(2,1)}) %all-gather.13.cloned.1.call-update) | async-done | bytes 1048592 | tf_op jit(solution)/shard_map/all_gather | solution.py:89
  67.6 2.3 copy.67
  69.8 3.4 all-to-all-done.4
  73.3 7.1 all-to-all-start.1
  80.5 38.5 %all-gather.11.cloned.1.call-done = bf16[128,4096]{1,0:T(8,128)(2,1)} async-done(((bf16[8,4096]{1,0:T(8,128)(2,1)}), bf16[128,4096]{1,0:T(8,128)(2,1)}) %all-gather.11.cloned.1.call-update) | async-done | bytes 1048592 | tf_op jit(solution)/shard_map/all_gather | solution.py:88
  119.0 2.3 copy.64
  121.4 6.8 all-to-all-start
  128.2 0.8 fusion.48
  129.1 41.4 %all-gather.17.cloned.1.call-done = bf16[128,4096]{1,0:T(8,128)(2,1)} async-done(((bf16[8,4096]{1,0:T(8,128)(2,1)}), bf16[128,4096]{1,0:T(8,128)(2,1)}) %all-gather.17.cloned.1.call-update) | async-done | bytes 1048592 | tf_op jit(solution)/shard_map/all_gather | solution.py:94
  170.5 2.3 copy.79
  172.8 6.9 all-to-all-start.5
  179.7 45.4 %all-gather.15.cloned.1.call-done = bf16[128,8192]{1,0:T(8,128)(2,1)} async-done(((bf16[8,8192]{1,0:T(8,128)(2,1)}), bf16[128,8192]{1,0:T(8,128)(2,1)}) %all-gather.15.cloned.1.call-update) | async-done | bytes 2097168 | tf_op jit(solution)/shard_map/all_gather | solution.py:90
  225.1 4.1 copy.70
  229.2 6.8 all-to-all-start.2
  237.8 1.1 copy.74
  238.9 2.4 copy.68
  241.3 2.3 copy.69
  243.6 1.3 copy.65
  244.9 2.4 copy.66
  247.2 1.5 copy.80
  248.7 1.1 copy.81
  249.8 48.6 %all-to-all-done.2 = bf16[128,16,512]{0,2,1:T(8,128)(2,1)S(1)} async-done(((bf16[128,16,512]{0,2,1:T(8,128)(2,1)}), bf16[128,16,512]{0,2,1:T(8,128)(2,1)S(1)}, u32[]{:S(2)}, u32[]{:S(2)}) %all-to-all-start.2) | async-done | bytes 2097184 | tf_op jit(solution)/shard_map/all_to_all | solution.py:101
  298.4 2.6 copy.71
  301.1 1.9 copy.72
  303.0 54.4 %all-gather.9.cloned.1.call-done = bf16[1024,2048]{1,0:T(8,128)(2,1)} async-done(((bf16[64,2048]{1,0:T(8,128)(2,1)}), bf16[1024,2048]{1,0:T(8,128)(2,1)}) %all-gather.9.cloned.1.call-update) | async-done | bytes 4194320 | tf_op jit(solution)/shard_map/all_gather | solution.py:113
  357.3 9.9 %fusion.85 = (bf16[1024,1280]{1,0:T(8,128)(2,1)}, f32[1024,1280]{1,0:T(8,128)S(1)}) fusion(bf16[1024,2048]{1,0:T(8,128)(2,1)} %all-gather.9.cloned.1.call-done, bf16[2048,256]{1,0:T(8,128)(2,1)S(1)} %bitcast.113, bf16[2048,512]{1,0:T(8,128)(2,1)S(1)} %bitcast.111, bf16[2048,256]{1,0:T(8,128)(2,1)} %bitcast.114, bf16[2048,256]{1,0:T(8,128)(2,1)} %bitcast.115), kind=kOutput, calls=%fused_computation.126 | convolution fusion | flops 5390991360 | bytes 17301504 | tf_op jit(solution)/shard_map/dot_general | solution.py:115
  367.2 1.2 fusion.84
  368.4 1.4 copy-done.5
  370.8 0.8 slice_negate_fusion
  371.6 0.9 pad_maximum_fusion.2
  372.6 0.7 reshape.454
  373.7 1.6 copy.75
  375.9 0.8 slice_negate_fusion.1
  376.7 0.9 pad_maximum_fusion.1
  377.6 0.7 reshape.452
  378.7 7.1 fusion.25
  385.9 0.8 copy-done.11
  386.8 1.7 convolution_bitcast_fusion.1
  388.5 2.7 convolution_bitcast_fusion
  391.6 4.5 convolution_convert_fusion
  396.1 0.8 copy-done.14
  398.4 96.7 %reduce-scatter.2.cloned.1.call-done = bf16[64,2048]{1,0:T(8,128)(2,1)} async-done(((bf16[1024,2048]{1,0:T(8,128)(2,1)}), bf16[64,2048]{1,0:T(8,128)(2,1)}) %reduce-scatter.2.cloned.1.call-update) | async-done | bytes 262160 | tf_op jit(solution)/shard_map/reduce_scatter | solution.py:164
  495.1 1.1 fusion.43
  496.3 0.7 copy-done.10
  497.0 0.8 fusion.45
  497.9 51.9 %all-gather.21.cloned.1.call-done = bf16[128,4096]{1,0:T(8,128)(2,1)} async-done(((bf16[8,4096]{1,0:T(8,128)(2,1)}), bf16[128,4096]{1,0:T(8,128)(2,1)}) %all-gather.21.cloned.1.call-update) | async-done | bytes 1048592 | tf_op jit(solution)/shard_map/all_gather | solution.py:95
  549.8 2.3 copy.82
  552.1 6.8 all-to-all-start.6
  558.9 42.4 %all-gather.23.cloned.1.call-done = bf16[128,4096]{1,0:T(8,128)(2,1)} async-done(((bf16[8,4096]{1,0:T(8,128)(2,1)}), bf16[128,4096]{1,0:T(8,128)(2,1)}) %all-gather.23.cloned.1.call-update) | async-done | bytes 1048592 | tf_op jit(solution)/shard_map/all_gather | solution.py:96
  601.3 2.3 copy.85
  603.6 6.8 all-to-all-start.7
  611.0 1.1 copy.84
  612.1 31.6 %all-to-all-done.7 = bf16[128,16,256]{0,2,1:T(8,128)(2,1)S(1)} async-done(((bf16[128,16,256]{0,2,1:T(8,128)(2,1)}), bf16[128,16,256]{0,2,1:T(8,128)(2,1)S(1)}, u32[]{:S(2)}, u32[]{:S(2)}) %all-to-all-start.7) | async-done | bytes 1048608 | tf_op jit(solution)/shard_map/all_to_all | solution.py:105
  644.3 69.9 %all-gather.19.cloned.1.call-done = bf16[1024,2048]{1,0:T(8,128)(2,1)} async-done(((bf16[64,2048]{1,0:T(8,128)(2,1)}), bf16[1024,2048]{1,0:T(8,128)(2,1)}) %all-gather.19.cloned.1.call-update) | async-done | bytes 4194320 | tf_op jit(solution)/shard_map/all_gather | solution.py:177
  714.2 4.5 fusion.8
  718.7 1.1 fusion.32
  (88 shorter events, 8.5 us)
Async XLA Ops:
  7.2 229.0 %copy-start = (f32[1024,8]{0,1:T(8,128)S(1)}, f32[1024,8]{0,1:T(8,128)}, u32[]{:S(2)}) copy-start(f32[1024,8]{0,1:T(8,128)} %param.16) | copy-start | bytes 98308
  7.2 60.4 %all-gather.13.cloned.1.call-start = ((), (), s32[]{:S(2)}) async-start(), calls=%async_computation.11 | async-start | bytes 1114112 | tf_op jit(solution)/shard_map/all_gather | solution.py:89
  8.7 110.3 %all-gather.11.cloned.1.call-start = ((), (), s32[]{:S(2)}) async-start(), calls=%async_computation.10 | async-start | bytes 1114112 | tf_op jit(solution)/shard_map/all_gather | solution.py:88
  10.3 160.2 %all-gather.17.cloned.1.call-start = ((), (), s32[]{:S(2)}) async-start(), calls=%async_computation.13 | async-start | bytes 1114112 | tf_op jit(solution)/shard_map/all_gather | solution.py:94
  39.0 9.7 %copy-start.13 = (f32[8,4096]{1,0:T(8,128)S(1)}, f32[8,4096]{1,0:T(8,128)}, u32[]{:S(2)}) copy-start(f32[8,4096]{1,0:T(8,128)} %param.19) | copy-start | bytes 393220
  40.4 32.9 %all-to-all-start.4 = ((bf16[128,16,256]{2,0,1:T(8,128)(2,1)}), bf16[128,16,256]{2,0,1:T(8,128)(2,1)S(1)}, u32[]{:S(2)}, u32[]{:S(2)}) async-start(bf16[128,16,256]{2,0,1:T(8,128)(2,1)} %copy.73), calls=%async_computation.4 | async-start | bytes 2097152 | tf_op jit(solution)/shard_map/all_to_all | solution.py:102
  48.7 31.7 %copy-start.6 = (bf16[64,2048]{1,0:T(8,128)(2,1)S(1)}, bf16[64,2048]{1,0:T(8,128)(2,1)}, u32[]{:S(2)}) copy-start(bf16[64,2048]{1,0:T(8,128)(2,1)} %param.12) | copy-start | bytes 786436
  48.7 176.4 %all-gather.15.cloned.1.call-start = ((), (), s32[]{:S(2)}) async-start(), calls=%async_computation.12 | async-start | bytes 2228224 | tf_op jit(solution)/shard_map/all_gather | solution.py:90
  73.3 48.1 %all-to-all-start.1 = ((bf16[128,16,256]{0,2,1:T(8,128)(2,1)}), bf16[128,16,256]{0,2,1:T(8,128)(2,1)S(1)}, u32[]{:S(2)}, u32[]{:S(2)}) async-start(bf16[128,16,256]{0,2,1:T(8,128)(2,1)} %bitcast.10), calls=%async_computation.1 | async-start | bytes 2097152 | tf_op jit(solution)/shard_map/all_to_all | solution.py:100
  80.4 47.9 %copy-start.16 = (f32[2048]{0:T(1024)S(1)}, f32[2048]{0:T(1024)}, u32[]{:S(2)}) copy-start(f32[2048]{0:T(1024)} %param.13) | copy-start | bytes 24580
  121.4 51.4 %copy-start.2 = (bf16[128,16,256]{0,2,1:T(8,128)(2,1)}, bf16[128,16,256]{0,2,1:T(8,128)(2,1)S(1)}, u32[]{:S(2)}) copy-start(bf16[128,16,256]{0,2,1:T(8,128)(2,1)S(1)} %all-to-all-done.1) | copy-start | bytes 3145732
  121.4 51.4 %all-to-all-start = ((bf16[128,16,256]{0,2,1:T(8,128)(2,1)}), bf16[128,16,256]{0,2,1:T(8,128)(2,1)S(1)}, u32[]{:S(2)}, u32[]{:S(2)}) async-start(bf16[128,16,256]{0,2,1:T(8,128)(2,1)} %bitcast.100), calls=%async_computation | async-start | bytes 2097152 | tf_op jit(solution)/shard_map/all_to_all | solution.py:99
  128.2 229.1 %all-gather.9.cloned.1.call-start = ((), (), s32[]{:S(2)}) async-start(), calls=%async_computation.9 | async-start | bytes 4456448 | tf_op jit(solution)/shard_map/all_gather | solution.py:113
  172.8 56.5 %copy-start.3 = (bf16[128,16,256]{0,2,1:T(8,128)(2,1)}, bf16[128,16,256]{0,2,1:T(8,128)(2,1)S(1)}, u32[]{:S(2)}) copy-start(bf16[128,16,256]{0,2,1:T(8,128)(2,1)S(1)} %all-to-all-done) | copy-start | bytes 3145732
  172.8 56.5 %all-to-all-start.5 = ((bf16[128,16,256]{0,2,1:T(8,128)(2,1)}), bf16[128,16,256]{0,2,1:T(8,128)(2,1)}, u32[]{:S(2)}, u32[]{:S(2)}) async-start(bf16[128,16,256]{0,2,1:T(8,128)(2,1)} %bitcast.102), calls=%async_computation.5 | async-start | bytes 2097152 | tf_op jit(solution)/shard_map/all_to_all | solution.py:103
  229.2 69.2 %all-to-all-start.2 = ((bf16[128,16,512]{0,2,1:T(8,128)(2,1)}), bf16[128,16,512]{0,2,1:T(8,128)(2,1)S(1)}, u32[]{:S(2)}, u32[]{:S(2)}) async-start(bf16[128,16,512]{0,2,1:T(8,128)(2,1)} %bitcast.17), calls=%async_computation.2 | async-start | bytes 4194304 | tf_op jit(solution)/shard_map/all_to_all | solution.py:101
  236.1 259.1 %reduce-scatter.2.cloned.1.call-start = ((), (), s32[]{:S(2)}) async-start(), calls=%async_computation.14 | async-start | bytes 4456448 | tf_op jit(solution)/shard_map/reduce_scatter | solution.py:164
  238.9 4.7 copy-start.4
  301.1 56.3 %copy-start.8 = (bf16[16,16,8,256]{3,2,1,0:T(8,128)(2,1)S(1)}, bf16[16,16,8,256]{3,2,1,0:T(8,128)(2,1)}, u32[]{:S(2)}) copy-start(bf16[16,16,8,256]{3,2,1,0:T(8,128)(2,1)} %copy.74) | copy-start | bytes 3145732
  367.2 2.7 copy-start.5
  385.8 0.8 copy-start.11
  385.8 1.0 copy-start.12
  388.5 3.1 copy-start.7
  396.1 0.9 copy-start.14
  396.1 1.6 copy-start.15
  396.1 100.9 %copy-start.17 = (f32[2048]{0:T(1024)S(1)}, f32[2048]{0:T(1024)}, u32[]{:S(2)}) copy-start(f32[2048]{0:T(1024)} %param.14) | copy-start | bytes 24580
  396.1 153.7 %all-gather.21.cloned.1.call-start = ((), (), s32[]{:S(2)}) async-start(), calls=%async_computation.16 | async-start | bytes 1114112 | tf_op jit(solution)/shard_map/all_gather | solution.py:95
  397.6 203.7 %all-gather.23.cloned.1.call-start = ((), (), s32[]{:S(2)}) async-start(), calls=%async_computation.17 | async-start | bytes 1114112 | tf_op jit(solution)/shard_map/all_gather | solution.py:96
  398.4 315.8 %all-gather.19.cloned.1.call-start = ((), (), s32[]{:S(2)}) async-start(), calls=%async_computation.15 | async-start | bytes 4456448 | tf_op jit(solution)/shard_map/all_gather | solution.py:177
  496.3 0.7 copy-start.10
  552.1 51.5 %all-to-all-start.6 = ((bf16[128,16,256]{0,2,1:T(8,128)(2,1)}), bf16[128,16,256]{0,2,1:T(8,128)(2,1)S(1)}, u32[]{:S(2)}, u32[]{:S(2)}) async-start(bf16[128,16,256]{0,2,1:T(8,128)(2,1)} %bitcast.45), calls=%async_computation.7 | async-start | bytes 2097152 | tf_op jit(solution)/shard_map/all_to_all | solution.py:104
  603.6 40.1 %all-to-all-start.7 = ((bf16[128,16,256]{0,2,1:T(8,128)(2,1)}), bf16[128,16,256]{0,2,1:T(8,128)(2,1)S(1)}, u32[]{:S(2)}, u32[]{:S(2)}) async-start(bf16[128,16,256]{0,2,1:T(8,128)(2,1)} %bitcast.50), calls=%async_computation.8 | async-start | bytes 2097152 | tf_op jit(solution)/shard_map/all_to_all | solution.py:105
  612.1 102.2 %copy-start.9 = (bf16[16,16,8,256]{3,2,1,0:T(8,128)(2,1)S(1)}, bf16[16,16,8,256]{3,2,1,0:T(8,128)(2,1)}, u32[]{:S(2)}) copy-start(bf16[16,16,8,256]{3,2,1,0:T(8,128)(2,1)} %copy.84) | copy-start | bytes 3145732
  714.2 5.6 copy-start.1
Sparse Core Ops, SparseCore 0:
  11.3 56.1 all-gather.12
  70.3 48.6 all-gather.10
  121.8 48.6 all-gather.16
  173.7 51.4 all-gather.14
  227.3 129.9 all-gather.8
  396.2 98.8 reduce-scatter.1
  497.9 51.8 all-gather.20
  552.6 48.6 all-gather.22
  603.6 110.5 all-gather.18
